TPU v7x, 128 devices: a whole 4x4x4 slice. The times are simulated.
128 devices in a mesh: dp: 8 (over x, core), tp: 16 (over y, z).
Axes of the slice: x: 4, y: 4, z: 4, core: 2. Of those that a mesh axis runs over, the one named last changes fastest.
Arguments:
- queries: bfloat16 [1024, 128, 576], P(('dp', 'tp')), may hold values from -10 to 10
- new_latent: bfloat16 [1024, 576], P(('dp', 'tp')), may hold values from -6 to 6
- resident: bfloat16 [768, 256, 576], P(('dp', 'tp')), may hold values from -6 to 6
- leaving: bfloat16 [256, 2, 256, 576], P(('dp', 'tp')), may hold values from -6 to 6
- res_len: int32 [768], P(('dp', 'tp')), may hold values from 1 to 256, as said below
- leave_len: int32 [128, 2], replicated, may hold values from 1 to 256, as said below
- mig_dest: int32 [128, 2], replicated, may hold values from 0 to 15, as said below
- stream: bfloat16 [1024, 7168], P(('dp', 'tp')), may hold values from -6 to 6
- dense_gain: float32 [7168], replicated, may hold values from 0.1 to 1.9
- w_gate: bfloat16 [7168, 18432], P('dp', 'tp'), may hold values from -0.0625 to 0.0625
- w_up: bfloat16 [7168, 18432], P('dp', 'tp'), may hold values from -0.0625 to 0.0625
- w_down: bfloat16 [18432, 7168], P('tp', 'dp'), may hold values from -0.046875 to 0.046875
- moe_gain: float32 [7168], replicated, may hold values from 0.1 to 1.9
- expert_gate: bfloat16 [16, 7168, 2048], P('tp', None, 'dp'), may hold values from -0.0625 to 0.0625
- expert_up: bfloat16 [16, 7168, 2048], P('tp', None, 'dp'), may hold values from -0.0625 to 0.0625
- expert_down: bfloat16 [16, 2048, 7168], P('tp', 'dp'), may hold values from -0.125 to 0.125
- expert_ids: int32 [1024, 8], P(('dp', 'tp')), may hold values from 0 to 15, all different within a row; in each aligned block of 8 rows (0 to 7, 8 to 15, ...) at most 5 rows name the same one
- gate_scores: float32 [1024, 8], P(('dp', 'tp')), may hold values from 0.05 to 1
Outputs:
- context: bfloat16 [1024, 128, 512], P(('dp', 'tp'))
- arrived: bfloat16 [256, 2, 256, 576], P(('dp', 'tp'))
- stream_out: bfloat16 [1024, 7168], P(('dp', 'tp'))
Inputs may be any that keep to these rules, and one draw needn't show every extreme that they name: `mig_dest`: each device sends its 2 leaving requests to 2 different other devices of its dp index, and every device receives exactly 2 requests. `res_len`: some request holds all 256 positions. `leave_len`: some request holds all 256 positions. `expert_ids`: among the 8 rows of one device no expert is chosen by more than 5 rows, a bound that some block reaches; a row names 8 different experts.
All inputs are finite; a program needn't handle non-finite values.
Results may differ from a plain program's by a relative error of at most 0.023.
Values may be sent and summed in bfloat16 or wider, within the bound.
A program may use at most 128 MiB of HBM per device.

v0:
```python
import jax
import jax.numpy as jnp
from jax import lax
from jax.sharding import PartitionSpec as P

VDIM = 512
QKD = 192
EPS = 1e-06
ROUTE_SCALE = 2.5


def rms_scale(rows, gain):
    values = rows.astype(jnp.float32)
    mean_square = jnp.mean(values * values, axis=-1, keepdims=True)
    return (values * lax.rsqrt(mean_square + EPS) * gain).astype(jnp.bfloat16)


def attend(queries, keys, lengths, newest):
    scale = QKD ** (-0.5)
    scores = jnp.einsum("rhl,rcl->rhc", queries, keys, preferred_element_type=jnp.float32) * scale
    positions = jnp.arange(keys.shape[1])
    valid = positions[None, None, :] < lengths[:, None, None]
    masked = jnp.where(valid, scores, -1e30)
    own_score = (
        jnp.einsum("rhl,rl->rh", queries, newest, preferred_element_type=jnp.float32) * scale
    )
    top = jnp.maximum(jnp.max(masked, axis=-1), own_score)
    expo = jnp.where(valid, jnp.exp(masked - top[..., None]), 0.0)
    own_expo = jnp.exp(own_score - top)
    total = jnp.sum(expo, axis=-1) + own_expo
    weights = (expo / total[..., None]).astype(jnp.bfloat16)
    own_weight = (own_expo / total).astype(jnp.bfloat16)
    context = jnp.einsum(
        "rhc,rcv->rhv", weights, keys[:, :, :VDIM], preferred_element_type=jnp.float32
    )
    context = context + own_weight.astype(jnp.float32)[..., None] * newest[:, None, :VDIM].astype(
        jnp.float32
    )
    return context.astype(jnp.bfloat16)


def on_device(
    queries,
    new_latent,
    resident,
    leaving,
    res_len,
    leave_len,
    mig_dest,
    stream,
    dense_gain,
    w_gate,
    w_up,
    w_down,
    moe_gain,
    expert_gate,
    expert_up,
    expert_down,
    expert_ids,
    gate_scores,
):
    tp_count = lax.axis_size("tp")
    dp_count = lax.axis_size("dp")
    tp_rank = lax.axis_index("tp")
    dp_rank = lax.axis_index("dp")
    moving = leaving.shape[0]
    device = dp_rank * tp_count + tp_rank
    peers = jnp.arange(tp_count)
    own_dest = lax.dynamic_index_in_dim(mig_dest, device, 0, keepdims=False)
    outgoing = jnp.zeros((tp_count,) + leaving.shape[1:], jnp.bfloat16)
    for slot in range(moving):
        outgoing = jnp.where(
            (peers == own_dest[slot])[:, None, None, None], leaving[slot][None], outgoing
        )
    incoming = lax.all_to_all(outgoing, "tp", split_axis=0, concat_axis=0, tiled=True)
    group_dest = lax.dynamic_slice_in_dim(mig_dest, dp_rank * tp_count, tp_count, 0)
    group_len = lax.dynamic_slice_in_dim(leave_len, dp_rank * tp_count, tp_count, 0)
    match = group_dest == tp_rank
    is_source = jnp.any(match, axis=1)
    which = jnp.sum(jnp.where(match, jnp.arange(moving)[None, :], 0), axis=1)
    order = jnp.cumsum(is_source.astype(jnp.int32)) - 1
    arrivals = []
    arrival_len = []
    for arrival in range(moving):
        pick = is_source & (order == arrival)
        source = jnp.sum(jnp.where(pick, peers, 0))
        slot = jnp.sum(jnp.where(pick, which, 0))
        arrivals.append(lax.dynamic_index_in_dim(incoming, source, 0, keepdims=False))
        source_len = lax.dynamic_index_in_dim(group_len, source, 0, keepdims=False)
        arrival_len.append(lax.dynamic_index_in_dim(source_len, slot, 0, keepdims=False))
    arrived = jnp.stack(arrivals, axis=0)
    arrived_len = jnp.stack(arrival_len, axis=0)
    stay = resident.shape[0]
    context_stay = attend(queries[:stay], resident, res_len, new_latent[:stay])
    context_moved = attend(queries[stay:], arrived[:, 0], arrived_len, new_latent[stay:])
    context = jnp.concatenate([context_stay, context_moved], axis=0)
    rows_dev = stream.shape[0]
    width = stream.shape[1]
    normed = rms_scale(stream, dense_gain)
    nearby = lax.all_gather(normed[None], "tp", axis=0, tiled=True)
    gathered = lax.all_to_all(nearby[:, None], "dp", split_axis=3, concat_axis=1, tiled=True)
    features = gathered.reshape(-1, gathered.shape[-1])
    gate_part = jnp.dot(features, w_gate, preferred_element_type=jnp.float32)
    up_part = jnp.dot(features, w_up, preferred_element_type=jnp.float32)
    gate, up = (
        lax.psum(gate_part.astype(jnp.bfloat16), "dp").astype(jnp.float32),
        lax.psum(up_part.astype(jnp.bfloat16), "dp").astype(jnp.float32),
    )
    hidden_all = (jax.nn.silu(gate) * up).astype(jnp.bfloat16)
    block = hidden_all
    ffn_share = lax.psum_scatter(
        jnp.dot(block, w_down, preferred_element_type=jnp.float32).astype(jnp.bfloat16),
        "tp",
        scatter_dimension=0,
        tiled=True,
    ).astype(jnp.float32)
    ffn_rows = lax.all_to_all(
        ffn_share.reshape(dp_count, rows_dev, ffn_share.shape[-1]).astype(jnp.bfloat16),
        "dp",
        split_axis=0,
        concat_axis=2,
        tiled=True,
    ).astype(jnp.float32)
    middle = (stream.astype(jnp.float32) + ffn_rows[0]).astype(jnp.bfloat16)
    mixed = rms_scale(middle, moe_gain)
    experts = expert_gate.shape[0] * tp_count
    top_count = expert_ids.shape[1]
    capacity = min(rows_dev, rows_dev * top_count // experts + 1)
    hits = (expert_ids[:, :, None] == jnp.arange(experts)[None, None, :]).astype(jnp.int32)
    row_hits = jnp.sum(hits, axis=1)
    before = jnp.cumsum(row_hits, axis=0) - row_hits
    slot_of = jnp.sum(hits * before[:, None, :], axis=2)
    target = expert_ids * capacity + slot_of
    placed = jnp.any(target[:, :, None] == jnp.arange(experts * capacity)[None, None, :], axis=1)
    outgoing_rows = jnp.dot(
        placed.T.astype(jnp.bfloat16), mixed, preferred_element_type=jnp.float32
    )
    outgoing_rows = outgoing_rows.astype(jnp.bfloat16).reshape(experts, capacity, width)
    received = lax.all_to_all(outgoing_rows, "tp", split_axis=0, concat_axis=0, tiled=True)
    pooled = lax.all_gather(received, "dp", axis=0, tiled=True)
    flat = pooled.reshape(-1, width)
    block = flat
    gate = jnp.dot(block, expert_gate[0], preferred_element_type=jnp.float32)
    up = jnp.dot(block, expert_up[0], preferred_element_type=jnp.float32)
    inner = (jax.nn.silu(gate) * up).astype(jnp.bfloat16)
    summed = lax.psum_scatter(
        jnp.dot(inner, expert_down[0], preferred_element_type=jnp.float32).astype(jnp.bfloat16),
        "dp",
        scatter_dimension=0,
        tiled=True,
    )
    results = summed.reshape(received.shape)
    returned = lax.all_to_all(results, "tp", split_axis=0, concat_axis=0, tiled=True)
    flat_back = returned.reshape(experts * capacity, width)
    picked = jnp.take(flat_back, target.reshape(-1), axis=0).reshape(rows_dev, top_count, width)
    shares = gate_scores / jnp.sum(gate_scores, axis=1, keepdims=True) * ROUTE_SCALE
    routed = jnp.einsum("rk,rkd->rd", shares, picked.astype(jnp.float32))
    stream_out = (middle.astype(jnp.float32) + routed).astype(jnp.bfloat16)
    return (context, arrived, stream_out)


def solution(mesh):
    placed = (
        P(("dp", "tp"), None, None),
        P(("dp", "tp"), None),
        P(("dp", "tp"), None, None),
        P(("dp", "tp"), None, None, None),
        P(("dp", "tp")),
        P(),
        P(),
        P(("dp", "tp"), None),
        P(),
        P("dp", "tp"),
        P("dp", "tp"),
        P("tp", "dp"),
        P(),
        P("tp", None, "dp"),
        P("tp", None, "dp"),
        P("tp", "dp", None),
        P(("dp", "tp"), None),
        P(("dp", "tp"), None),
    )
    return jax.shard_map(
        on_device,
        mesh=mesh,
        in_specs=placed,
        out_specs=(
            P(("dp", "tp"), None, None),
            P(("dp", "tp"), None, None, None),
            P(("dp", "tp"), None),
        ),
        check_vma=False,
    )
```

profile of v0, /device:TPU:0, one launch (start us, length us, event | category | flops | bytes accessed | tf_op | source)
XLA Modules:
  0.0 688.6 jit_solution(10923640459823760998)
XLA Ops:
  8.4 1.6 fusion.51
  10.2 47.7 %all-gather.6.cloned.1.call-done = bf16[128,7168]{1,0:T(8,128)(2,1)} async-done(((bf16[8,7168]{1,0:T(8,128)(2,1)}), bf16[128,7168]{1,0:T(8,128)(2,1)}) %all-gather.6.cloned.1.call-update) | async-done | bytes 1835024 | tf_op jit(solution)/shard_map/all_gather | solution.py:100
  57.8 13.7 %copy.81 = bf16[16,1,8,7168]{0,2,1,3:T(8,128)(2,1)} copy(bf16[16,1,8,7168]{3,2,0,1:T(8,128)(2,1)} %bitcast.99) | data formatting | bytes 3670016 | tf_op jit(solution)/shard_map/broadcast_in_dim | solution.py:101
  71.6 17.3 %reshape.231 = bf16[8,2,57344]{2,1,0:T(2,128)(2,1)} reshape(bf16[7168,1,8,16]{3,2,1,0:T(8,128)(2,1)} %bitcast.94) | data formatting | bytes 3670016
  88.8 28.8 %all_to_all.39 = bf16[8,2,57344]{2,1,0:T(2,128)(2,1)} all-to-all(bf16[8,2,57344]{2,1,0:T(2,128)(2,1)} %reshape.231), channel_id=1, replica_groups=mesh['dp'=8,'tp'=16] {'dp'}, dimensions={0} | all-to-all | bytes 3670016 | tf_op jit(solution)/shard_map/all_to_all | solution.py:101
  117.6 12.5 %reshape.232 = bf16[7168,1,8,16]{3,2,1,0:T(8,128)(2,1)} reshape(bf16[8,2,57344]{2,1,0:T(2,128)(2,1)} %all_to_all.39) | data formatting | bytes 3670016
  130.1 13.8 %copy.95 = bf16[16,1,8,8,896]{4,3,2,0,1:T(8,128)(2,1)} copy(bf16[16,1,8,8,896]{0,2,4,3,1:T(8,128)(2,1)} %bitcast.95) | data formatting | bytes 3670016 | tf_op jit(solution)/shard_map/all_to_all | solution.py:101
  143.9 1.8 copy.83
  145.8 4.1 convolution_convert_fusion.2
  149.8 4.1 convolution_convert_fusion.3
  154.0 71.9 %all-reduce.3.cloned.1.call-done = (bf16[1024,1152]{1,0:T(8,128)(2,1)}, bf16[1024,1152]{1,0:T(8,128)(2,1)}) async-done(((bf16[1024,1152]{1,0:T(8,128)(2,1)}, bf16[1024,1152]{1,0:T(8,128)(2,1)}), (bf16[1024,1152]{1,0:T(8,128)(2,1)}, bf16[1024,1152]{1,0:T(8,128)(2,1)})) %all-reduce.3.cloned.1.call-update) | async-done | bytes 4718608 | tf_op jit(solution)/shard_map/psum | solution.py:107
  225.9 7.3 %fusion.12 = bf16[1024,896]{1,0:T(8,128)(2,1)} fusion(bf16[1152,896]{1,0:T(8,128)(2,1)} %param.29, bf16[1024,1152]{1,0:T(8,128)(2,1)} %get-tuple-element.30, bf16[1024,1152]{1,0:T(8,128)(2,1)} %get-tuple-element.31), kind=kOutput, calls=%fused_computation.19 | convolution fusion | flops 2124283904 | bytes 8617984 | tf_op jit(solution)/shard_map/dot_general | solution.py:112
  233.7 75.1 %reduce-scatter.3.cloned.1.call-done = bf16[64,896]{1,0:T(8,128)(2,1)} async-done(((bf16[1024,896]{1,0:T(8,128)(2,1)}), bf16[64,896]{1,0:T(8,128)(2,1)}) %reduce-scatter.3.cloned.1.call-update) | async-done | bytes 114704 | tf_op jit(solution)/shard_map/reduce_scatter | solution.py:111
  308.7 4.3 all-to-all-start.2
  313.3 5.6 all-to-all-done.2
  320.2 29.9 %all_to_all.40 = bf16[16,5,7168]{2,1,0:T(8,128)(2,1)S(1)} all-to-all(bf16[16,5,7168]{2,1,0:T(8,128)(2,1)S(1)} %reshape.205), channel_id=1, replica_groups=mesh['dp'=8,'tp'=16] {'tp'}, dimensions={0} | all-to-all | bytes 2293760 | tf_op jit(solution)/shard_map/all_to_all | solution.py:139
  350.2 1.8 copy.84
  352.0 49.3 %all-gather.4.cloned.1.call-done = bf16[128,5,7168]{2,0,1:T(8,128)(2,1)} async-done(((bf16[16,5,7168]{2,0,1:T(8,128)(2,1)}), bf16[128,5,7168]{2,0,1:T(8,128)(2,1)}) %all-gather.4.cloned.1.call-update) | async-done | bytes 9175056 | tf_op jit(solution)/shard_map/all_gather | solution.py:140
  401.3 14.0 %copy.85 = bf16[128,5,7168]{2,1,0:T(8,128)(2,1)} copy(bf16[128,5,7168]{2,0,1:T(8,128)(2,1)} %all-gather.4.cloned.1.call-done) | data formatting | bytes 18350080 | tf_op jit(solution)/shard_map/all_gather | solution.py:140
  415.3 15.1 %reshape.206 = bf16[640,7168]{1,0:T(8,128)(2,1)} reshape(bf16[128,5,7168]{2,1,0:T(8,128)(2,1)} %copy.85) | data formatting | bytes 18350080 | tf_op jit(solution)/shard_map/reshape | solution.py:141
  430.4 7.2 %fusion.8 = f32[640,256]{1,0:T(8,128)S(1)} fusion(bf16[640,7168]{1,0:T(8,128)(2,1)} %reshape.206, bf16[1,7168,256]{2,1,0:T(8,128)(2,1)} %param.31), kind=kOutput, calls=%fused_computation.16 | convolution fusion | flops 2348810240 | bytes 13500416 | tf_op jit(solution)/shard_map/dot_general | solution.py:143
  437.6 18.9 %convolution_convert_fusion = bf16[640,7168]{1,0:T(8,128)(2,1)} fusion(bf16[1,256,7168]{2,1,0:T(8,128)(2,1)} %param.33, bf16[640,7168]{1,0:T(8,128)(2,1)} %reshape.206, bf16[1,7168,256]{2,1,0:T(8,128)(2,1)} %param.32, f32[640,256]{1,0:T(8,128)S(1)} %fusion.8), kind=kOutput, calls=%fused_computation.1 | convolution fusion | flops 4703191040 | bytes 26345472 | tf_op jit(solution)/shard_map/dot_general | solution.py:147
  459.1 4.9 select_select_fusion
  464.1 7.2 %all-to-all-start = ((bf16[16,2,256,576]{2,3,1,0:T(8,128)(2,1)}), bf16[16,2,256,576]{2,3,1,0:T(8,128)(2,1)}, u32[]{:S(2)}, u32[]{:S(2)}) async-start(bf16[16,2,256,576]{2,3,1,0:T(8,128)(2,1)} %select_select_fusion), calls=%async_computation | async-start | bytes 18874368 | tf_op jit(solution)/shard_map/all_to_all | solution.py:75
  482.3 2.2 fusion.88
  485.3 1.6 add_convert_fusion
  486.9 148.7 %all-to-all-done = bf16[16,2,256,576]{2,3,1,0:T(8,128)(2,1)} async-done(((bf16[16,2,256,576]{2,3,1,0:T(8,128)(2,1)}), bf16[16,2,256,576]{2,3,1,0:T(8,128)(2,1)}, u32[]{:S(2)}, u32[]{:S(2)}) %all-to-all-start) | async-done | bytes 9437216 | tf_op jit(solution)/shard_map/all_to_all | solution.py:75
  638.1 2.6 reshape.207
  640.7 10.5 %all-to-all-start.4 = ((bf16[16,5,7168]{2,1,0:T(8,128)(2,1)}), bf16[16,5,7168]{2,1,0:T(8,128)(2,1)S(1)}, u32[]{:S(2)}, u32[]{:S(2)}) async-start(bf16[16,5,7168]{2,1,0:T(8,128)(2,1)} %reshape.207), calls=%async_computation.6 | async-start | bytes 3670016 | tf_op jit(solution)/shard_map/all_to_all | solution.py:153
  654.1 23.0 %all-to-all-done.4 = bf16[16,5,7168]{2,1,0:T(8,128)(2,1)S(1)} async-done(((bf16[16,5,7168]{2,1,0:T(8,128)(2,1)}), bf16[16,5,7168]{2,1,0:T(8,128)(2,1)S(1)}, u32[]{:S(2)}, u32[]{:S(2)}) %all-to-all-start.4) | async-done | bytes 1146912 | tf_op jit(solution)/shard_map/all_to_all | solution.py:153
  677.7 2.1 gather_fusion
  679.7 1.6 fusion.31
  (101 shorter events, 17.0 us)
Async XLA Ops:
  7.2 138.6 %copy-start = (bf16[896,1152]{1,0:T(8,128)(2,1)S(1)}, bf16[896,1152]{1,0:T(8,128)(2,1)}, u32[]{:S(2)}) copy-start(bf16[896,1152]{1,0:T(8,128)(2,1)} %param.28) | copy-start | bytes 6193156
  7.2 50.6 %all-gather.6.cloned.1.call-start = ((), (), s32[]{:S(2)}) async-start(), calls=%async_computation.10 | async-start | bytes 1949696 | tf_op jit(solution)/shard_map/all_gather | solution.py:100
  10.1 215.8 %all-reduce.3.cloned.1.call-start = ((), (), s32[]{:S(2)}) async-start(), calls=%async_computation.11 | async-start | bytes 9437184 | tf_op jit(solution)/shard_map/psum | solution.py:107
  145.7 4.1 copy-start.16
  154.0 154.8 %reduce-scatter.3.cloned.1.call-start = ((), (), s32[]{:S(2)}) async-start(), calls=%async_computation.7 | async-start | bytes 1949696 | tf_op jit(solution)/shard_map/reduce_scatter | solution.py:111
  225.9 7.4 %copy-start.10 = (s32[8,8]{1,0:T(8,128)S(1)}, s32[8,8]{1,0:T(8,128)}, u32[]{:S(2)}) copy-start(s32[8,8]{1,0:T(8,128)} %param.34) | copy-start | bytes 772
  233.2 85.7 %copy-start.4 = (bf16[8,7168]{1,0:T(8,128)(2,1)S(1)}, bf16[8,7168]{1,0:T(8,128)(2,1)}, u32[]{:S(2)}) copy-start(bf16[8,7168]{1,0:T(8,128)(2,1)} %param.25) | copy-start | bytes 344068
  233.2 85.9 %copy-start.11 = (f32[7168]{0:T(1024)S(1)}, f32[7168]{0:T(1024)}, u32[]{:S(2)}) copy-start(f32[7168]{0:T(1024)} %param.30) | copy-start | bytes 86020
  308.7 10.2 %all-to-all-start.2 = ((bf16[8,8,896]{2,1,0:T(8,128)(2,1)}), bf16[8,8,896]{2,1,0:T(8,128)(2,1)S(1)}, u32[]{:S(2)}, u32[]{:S(2)}) async-start(bf16[8,8,896]{2,1,0:T(8,128)(2,1)} %bitcast.101), calls=%async_computation.3 | async-start | bytes 229376 | tf_op jit(solution)/shard_map/all_to_all | solution.py:117
  313.0 88.3 %all-gather.4.cloned.1.call-start = ((), (), s32[]{:S(2)}) async-start(), calls=%async_computation.8 | async-start | bytes 10321920 | tf_op jit(solution)/shard_map/all_gather | solution.py:140
  351.9 286.2 %reduce-scatter.5.cloned.1.call-start = ((), (), s32[]{:S(2)}) async-start(), calls=%async_computation.9 | async-start | bytes 10321920 | tf_op jit(solution)/shard_map/reduce_scatter | solution.py:146
  456.5 0.7 copy-start.13
  456.5 2.6 copy-start.3
  464.0 15.9 %copy-start.12 = (f32[8,8]{1,0:T(8,128)S(1)}, f32[8,8]{1,0:T(8,128)}, u32[]{:S(2)}) copy-start(f32[8,8]{1,0:T(8,128)} %param.35) | copy-start | bytes 772
  464.0 16.0 %copy-start.14 = (s32[128,2]{0,1:T(2,128)S(1)}, s32[128,2]{0,1:T(2,128)}, u32[]{:S(2)}) copy-start(s32[128,2]{0,1:T(2,128)} %param.23) | copy-start | bytes 3076
  464.0 18.0 %copy-start.15 = (s32[6]{0:T(128)S(1)}, s32[6]{0:T(128)}, u32[]{:S(2)}) copy-start(s32[6]{0:T(128)} %param.22) | copy-start | bytes 76
  464.0 18.1 %copy-start.9 = (bf16[8,576]{1,0:T(8,128)(2,1)S(1)}, bf16[8,576]{1,0:T(8,128)(2,1)}, u32[]{:S(2)}) copy-start(bf16[8,576]{1,0:T(8,128)(2,1)} %param.19) | copy-start | bytes 27652
  464.1 18.1 %copy-start.2 = (bf16[8,128,576]{1,2,0:T(8,128)(2,1)S(1)}, bf16[8,128,576]{1,2,0:T(8,128)(2,1)}, u32[]{:S(2)}) copy-start(bf16[8,128,576]{1,2,0:T(8,128)(2,1)} %param.18) | copy-start | bytes 3538948
  464.1 171.5 %all-to-all-start = ((bf16[16,2,256,576]{2,3,1,0:T(8,128)(2,1)}), bf16[16,2,256,576]{2,3,1,0:T(8,128)(2,1)}, u32[]{:S(2)}, u32[]{:S(2)}) async-start(bf16[16,2,256,576]{2,3,1,0:T(8,128)(2,1)} %select_select_fusion), calls=%async_computation | async-start | bytes 18874368 | tf_op jit(solution)/shard_map/all_to_all | solution.py:75
  482.3 2.9 copy-start.17
  637.0 3.7 copy-start.6
  640.7 36.4 %all-to-all-start.4 = ((bf16[16,5,7168]{2,1,0:T(8,128)(2,1)}), bf16[16,5,7168]{2,1,0:T(8,128)(2,1)S(1)}, u32[]{:S(2)}, u32[]{:S(2)}) async-start(bf16[16,5,7168]{2,1,0:T(8,128)(2,1)} %reshape.207), calls=%async_computation.6 | async-start | bytes 3670016 | tf_op jit(solution)/shard_map/all_to_all | solution.py:153
  651.2 1.2 copy-start.8
  651.2 1.4 copy-start.7
  651.3 1.8 copy-start.5
  677.7 4.4 copy-start.1
Sparse Core Ops, SparseCore 0:
  10.7 47.0 all-gather.5
  154.1 71.7 all-reduce.2
  233.4 75.3 reduce-scatter.2
  352.1 49.2 all-gather.3
  456.6 56.3 reduce-scatter.4
where the time goes:
time: 690 us; the launch traced here: 689 us
  waiting for transfers between devices  421 us (61%)
  local copies, waits for them, and re-layouts  100 us (14%)
  blocking collectives  58.7 us (9%)
  matrix products  49.5 us (7%)
  starting transfers between devices  22.3 us (3%)
  between operations  21.7 us (3%)
  other arithmetic  14.9 us (2%)
    all_to_all x1, waiting for transfers between devices, on_device(): lax.all_to_all(outgoing, 'tp', split_axis=0, concat_axis=0, tiled=True)  149 us
    reduce_scatter x1, waiting for transfers between devices, on_device(): lax.psum_scatter(jnp.dot(block, w_down, preferred_element_type=jnp.float3...  75.1 us
    psum x1, waiting for transfers between devices, on_device(): lax.psum(up_part.astype(jnp.bfloat16), 'dp').astype(jnp.float32)  71.9 us
    all_gather x1, waiting for transfers between devices, on_device(): pooled = lax.all_gather(received, 'dp', axis=0, tiled=True)  49.3 us
    all_gather x1, waiting for transfers between devices, on_device(): nearby = lax.all_gather(normed[None], 'tp', axis=0, tiled=True)  47.7 us
    unnamed x40, local copies, waits for them, and re-layouts  32.9 us
    all_to_all x1, blocking collectives, on_device(): lax.all_to_all(outgoing_rows, 'tp', split_axis=0, concat_axis=0, tiled=True)  29.9 us
    all_to_all x1, blocking collectives, on_device(): lax.all_to_all(nearby[:, None], 'dp', split_axis=3, concat_axis=1, tiled=...  28.8 us
  transfers between devices with their start and end apart: 8, of which 7 were waited for; matrix products, arithmetic and copies ran while one was open for 3% of the time, Pallas kernels for 0%

commit v1 on v0

--- a/solution.py
+++ b/solution.py
@@ -104,7 +104,7 @@
     up_part = jnp.dot(features, w_up, preferred_element_type=jnp.float32)
     gate, up = (
         lax.psum(gate_part.astype(jnp.bfloat16), "dp").astype(jnp.float32),
-        lax.psum(up_part.astype(jnp.bfloat16), "dp").astype(jnp.float32),
+        jnp.sum(lax.all_gather(up_part.astype(jnp.bfloat16), "dp"), axis=0).astype(jnp.float32),
     )
     hidden_all = (jax.nn.silu(gate) * up).astype(jnp.bfloat16)
     block = hidden_all

time: 690 us -> 776 us (1.12)
  waiting for transfers between devices: 421 us -> 491 us
  other arithmetic: 14.9 us -> 26.7 us
    all_gather x0 -> x1, waiting for transfers between devices: none -> 83.8 us  [on_device(): lax.all_gather(up_part.astype(jnp.bfloat16), 'dp')]
    psum x1, waiting for transfers between devices: 71.9 us -> 57.7 us  [on_device(): lax.psum(gate_part.astype(jnp.bfloat16), 'dp').astype(jnp.float32)]
    reduce_sum x0 -> x1, other arithmetic: none -> 11.9 us  [on_device(): jnp.sum(lax.all_gather(up_part.astype(jnp.bfloat16), 'dp'), axis=0)]
    unnamed x40 -> x42, local copies, waits for them, and re-layouts: 32.9 us -> 35.6 us
  transfers between devices with their start and end apart: 8 -> 9, of which waited for: 7 -> 8; matrix products, arithmetic and copies ran while one was open for 3% -> 5% of each run, Pallas kernels for 0% -> 0%
where the time goes in v1:
time: 776 us; the launch traced here: 774 us
  waiting for transfers between devices  491 us (63%)
  local copies, waits for them, and re-layouts  103 us (13%)
  blocking collectives  58.7 us (8%)
  matrix products  51.1 us (7%)
  other arithmetic  26.7 us (3%)
  starting transfers between devices  22.3 us (3%)
  between operations  22 us (3%)
    all_to_all x1, waiting for transfers between devices, on_device(): lax.all_to_all(outgoing, 'tp', split_axis=0, concat_axis=0, tiled=True)  149 us
    all_gather x1, waiting for transfers between devices, on_device(): lax.all_gather(up_part.astype(jnp.bfloat16), 'dp')  83.8 us
    reduce_scatter x1, waiting for transfers between devices, on_device(): lax.psum_scatter(jnp.dot(block, w_down, preferred_element_type=jnp.float3...  74.4 us
    psum x1, waiting for transfers between devices, on_device(): lax.psum(gate_part.astype(jnp.bfloat16), 'dp').astype(jnp.float32)  57.7 us
    all_gather x1, waiting for transfers between devices, on_device(): pooled = lax.all_gather(received, 'dp', axis=0, tiled=True)  49.3 us
    all_gather x1, waiting for transfers between devices, on_device(): nearby = lax.all_gather(normed[None], 'tp', axis=0, tiled=True)  47.7 us
    unnamed x42, local copies, waits for them, and re-layouts  35.6 us
    all_to_all x1, blocking collectives, on_device(): lax.all_to_all(outgoing_rows, 'tp', split_axis=0, concat_axis=0, tiled=True)  29.9 us
  transfers between devices with their start and end apart: 9, of which 8 were waited for; matrix products, arithmetic and copies ran while one was open for 5% of the time, Pallas kernels for 0%

profile of v1, /device:TPU:0, one launch (start us, length us, event | category | flops | bytes accessed | tf_op | source)
XLA Modules:
  0.0 774.3 jit_solution(12230703137019717061)
XLA Ops:
  8.4 1.6 fusion.51
  10.2 47.7 %all-gather.8.cloned.1.call-done = bf16[128,7168]{1,0:T(8,128)(2,1)} async-done(((bf16[8,7168]{1,0:T(8,128)(2,1)}), bf16[128,7168]{1,0:T(8,128)(2,1)}) %all-gather.8.cloned.1.call-update) | async-done | bytes 1835024 | tf_op jit(solution)/shard_map/all_gather | solution.py:100
  57.8 13.7 %copy.81 = bf16[16,1,8,7168]{0,2,1,3:T(8,128)(2,1)} copy(bf16[16,1,8,7168]{3,2,0,1:T(8,128)(2,1)} %bitcast.101) | data formatting | bytes 3670016 | tf_op jit(solution)/shard_map/broadcast_in_dim | solution.py:101
  71.6 17.3 %reshape.232 = bf16[8,2,57344]{2,1,0:T(2,128)(2,1)} reshape(bf16[7168,1,8,16]{3,2,1,0:T(8,128)(2,1)} %bitcast.95) | data formatting | bytes 3670016
  88.8 28.8 %all_to_all.39 = bf16[8,2,57344]{2,1,0:T(2,128)(2,1)} all-to-all(bf16[8,2,57344]{2,1,0:T(2,128)(2,1)} %reshape.232), channel_id=1, replica_groups=mesh['dp'=8,'tp'=16] {'dp'}, dimensions={0} | all-to-all | bytes 3670016 | tf_op jit(solution)/shard_map/all_to_all | solution.py:101
  117.6 12.5 %reshape.233 = bf16[7168,1,8,16]{3,2,1,0:T(8,128)(2,1)} reshape(bf16[8,2,57344]{2,1,0:T(2,128)(2,1)} %all_to_all.39) | data formatting | bytes 3670016
  130.1 13.8 %copy.95 = bf16[16,1,8,8,896]{4,3,2,0,1:T(8,128)(2,1)} copy(bf16[16,1,8,8,896]{0,2,4,3,1:T(8,128)(2,1)} %bitcast.96) | data formatting | bytes 3670016 | tf_op jit(solution)/shard_map/all_to_all | solution.py:101
  143.9 1.8 copy.83
  147.0 4.1 convolution_convert_fusion.2
  152.6 5.7 convolution_convert_fusion.3
  158.5 83.8 %all-gather.10.cloned.1.call-done = bf16[8192,1152]{1,0:T(8,128)(2,1)} async-done(((bf16[1024,1152]{1,0:T(8,128)(2,1)}), bf16[8192,1152]{1,0:T(8,128)(2,1)}) %all-gather.10.cloned.1.call-update) | async-done | bytes 18874384 | tf_op jit(solution)/shard_map/all_gather | solution.py:107
  242.3 11.9 %reduce_sum.128 = bf16[1024,1152]{1,0:T(8,128)(2,1)} reduce(bf16[8,1024,1152]{2,1,0:T(8,128)(2,1)} %bitcast.97, bf16[]{:T(256)} %constant.130.clone.1), dimensions={0}, to_apply=%region_13.14 | reduce | flops 8257536 | bytes 21233666 | tf_op jit(solution)/shard_map/reduce_sum | solution.py:107
  254.2 57.7 %all-reduce.2.cloned.1.call-done = bf16[1024,1152]{1,0:T(8,128)(2,1)} async-done(((bf16[1024,1152]{1,0:T(8,128)(2,1)}), bf16[1024,1152]{1,0:T(8,128)(2,1)}) %all-reduce.2.cloned.1.call-update) | async-done | bytes 2359312 | tf_op jit(solution)/shard_map/psum | solution.py:106
  311.9 7.3 fusion.12
  319.7 74.4 %reduce-scatter.3.cloned.1.call-done = bf16[64,896]{1,0:T(8,128)(2,1)} async-done(((bf16[1024,896]{1,0:T(8,128)(2,1)}), bf16[64,896]{1,0:T(8,128)(2,1)}) %reduce-scatter.3.cloned.1.call-update) | async-done | bytes 114704 | tf_op jit(solution)/shard_map/reduce_scatter | solution.py:111
  394.1 4.3 all-to-all-start.2
  398.5 5.8 all-to-all-done.2
  405.6 29.9 %all_to_all.40 = bf16[16,5,7168]{2,1,0:T(8,128)(2,1)S(1)} all-to-all(bf16[16,5,7168]{2,1,0:T(8,128)(2,1)S(1)} %reshape.205), channel_id=1, replica_groups=mesh['dp'=8,'tp'=16] {'tp'}, dimensions={0} | all-to-all | bytes 2293760 | tf_op jit(solution)/shard_map/all_to_all | solution.py:139
  435.6 1.8 copy.84
  437.4 49.3 %all-gather.6.cloned.1.call-done = bf16[128,5,7168]{2,0,1:T(8,128)(2,1)} async-done(((bf16[16,5,7168]{2,0,1:T(8,128)(2,1)}), bf16[128,5,7168]{2,0,1:T(8,128)(2,1)}) %all-gather.6.cloned.1.call-update) | async-done | bytes 9175056 | tf_op jit(solution)/shard_map/all_gather | solution.py:140
  486.7 14.0 %copy.85 = bf16[128,5,7168]{2,1,0:T(8,128)(2,1)} copy(bf16[128,5,7168]{2,0,1:T(8,128)(2,1)} %all-gather.6.cloned.1.call-done) | data formatting | bytes 18350080 | tf_op jit(solution)/shard_map/all_gather | solution.py:140
  500.7 15.1 %reshape.206 = bf16[640,7168]{1,0:T(8,128)(2,1)} reshape(bf16[128,5,7168]{2,1,0:T(8,128)(2,1)} %copy.85) | data formatting | bytes 18350080 | tf_op jit(solution)/shard_map/reshape | solution.py:141
  515.8 7.2 fusion.8
  523.0 18.9 %convolution_convert_fusion = bf16[640,7168]{1,0:T(8,128)(2,1)} fusion(bf16[1,256,7168]{2,1,0:T(8,128)(2,1)} %param.33, bf16[640,7168]{1,0:T(8,128)(2,1)} %reshape.206, bf16[1,7168,256]{2,1,0:T(8,128)(2,1)} %param.32, f32[640,256]{1,0:T(8,128)S(1)} %fusion.8), kind=kOutput, calls=%fused_computation.1 | convolution fusion | flops 4703191040 | bytes 26345472 | tf_op jit(solution)/shard_map/dot_general | solution.py:147
  544.5 4.9 select_select_fusion
  549.5 7.2 all-to-all-start
  567.8 2.2 fusion.88
  572.3 148.7 %all-to-all-done = bf16[16,2,256,576]{2,3,1,0:T(8,128)(2,1)} async-done(((bf16[16,2,256,576]{2,3,1,0:T(8,128)(2,1)}), bf16[16,2,256,576]{2,3,1,0:T(8,128)(2,1)}, u32[]{:S(2)}, u32[]{:S(2)}) %all-to-all-start) | async-done | bytes 9437216 | tf_op jit(solution)/shard_map/all_to_all | solution.py:75
  723.5 2.6 reshape.207
  726.1 10.5 %all-to-all-start.4 = ((bf16[16,5,7168]{2,1,0:T(8,128)(2,1)}), bf16[16,5,7168]{2,1,0:T(8,128)(2,1)S(1)}, u32[]{:S(2)}, u32[]{:S(2)}) async-start(bf16[16,5,7168]{2,1,0:T(8,128)(2,1)} %reshape.207), calls=%async_computation.6 | async-start | bytes 3670016 | tf_op jit(solution)/shard_map/all_to_all | solution.py:153
  739.5 23.0 %all-to-all-done.4 = bf16[16,5,7168]{2,1,0:T(8,128)(2,1)S(1)} async-done(((bf16[16,5,7168]{2,1,0:T(8,128)(2,1)}), bf16[16,5,7168]{2,1,0:T(8,128)(2,1)S(1)}, u32[]{:S(2)}, u32[]{:S(2)}) %all-to-all-start.4) | async-done | bytes 1146912 | tf_op jit(solution)/shard_map/all_to_all | solution.py:153
  763.1 2.1 gather_fusion
  (107 shorter events, 22.9 us)
Async XLA Ops:
  7.2 139.8 %copy-start = (bf16[896,1152]{1,0:T(8,128)(2,1)S(1)}, bf16[896,1152]{1,0:T(8,128)(2,1)}, u32[]{:S(2)}) copy-start(bf16[896,1152]{1,0:T(8,128)(2,1)} %param.28) | copy-start | bytes 6193156
  7.2 50.6 %all-gather.8.cloned.1.call-start = ((), (), s32[]{:S(2)}) async-start(), calls=%async_computation.11 | async-start | bytes 1949696 | tf_op jit(solution)/shard_map/all_gather | solution.py:100
  10.1 232.2 %all-gather.10.cloned.1.call-start = ((), (), s32[]{:S(2)}) async-start(), calls=%async_computation.12 | async-start | bytes 21233664 | tf_op jit(solution)/shard_map/all_gather | solution.py:107
  145.7 1.3 copy-start.3
  151.1 1.5 copy-start.4
  151.1 160.8 %all-reduce.2.cloned.1.call-start = ((), (), s32[]{:S(2)}) async-start(), calls=%async_computation.7 | async-start | bytes 4718592 | tf_op jit(solution)/shard_map/psum | solution.py:106
  158.3 235.9 %reduce-scatter.3.cloned.1.call-start = ((), (), s32[]{:S(2)}) async-start(), calls=%async_computation.8 | async-start | bytes 1949696 | tf_op jit(solution)/shard_map/reduce_scatter | solution.py:111
  254.2 65.1 %copy-start.12 = (s32[8,8]{1,0:T(8,128)S(1)}, s32[8,8]{1,0:T(8,128)}, u32[]{:S(2)}) copy-start(s32[8,8]{1,0:T(8,128)} %param.34) | copy-start | bytes 772
  319.2 85.1 %copy-start.6 = (bf16[8,7168]{1,0:T(8,128)(2,1)S(1)}, bf16[8,7168]{1,0:T(8,128)(2,1)}, u32[]{:S(2)}) copy-start(bf16[8,7168]{1,0:T(8,128)(2,1)} %param.25) | copy-start | bytes 344068
  319.2 85.3 %copy-start.13 = (f32[7168]{0:T(1024)S(1)}, f32[7168]{0:T(1024)}, u32[]{:S(2)}) copy-start(f32[7168]{0:T(1024)} %param.30) | copy-start | bytes 86020
  394.1 10.2 %all-to-all-start.2 = ((bf16[8,8,896]{2,1,0:T(8,128)(2,1)}), bf16[8,8,896]{2,1,0:T(8,128)(2,1)S(1)}, u32[]{:S(2)}, u32[]{:S(2)}) async-start(bf16[8,8,896]{2,1,0:T(8,128)(2,1)} %bitcast.103), calls=%async_computation.3 | async-start | bytes 229376 | tf_op jit(solution)/shard_map/all_to_all | solution.py:117
  398.4 88.4 %all-gather.6.cloned.1.call-start = ((), (), s32[]{:S(2)}) async-start(), calls=%async_computation.9 | async-start | bytes 10321920 | tf_op jit(solution)/shard_map/all_gather | solution.py:140
  437.3 286.2 %reduce-scatter.5.cloned.1.call-start = ((), (), s32[]{:S(2)}) async-start(), calls=%async_computation.10 | async-start | bytes 10321920 | tf_op jit(solution)/shard_map/reduce_scatter | solution.py:146
  541.9 0.7 copy-start.15
  541.9 2.6 copy-start.5
  549.4 15.9 %copy-start.14 = (f32[8,8]{1,0:T(8,128)S(1)}, f32[8,8]{1,0:T(8,128)}, u32[]{:S(2)}) copy-start(f32[8,8]{1,0:T(8,128)} %param.35) | copy-start | bytes 772
  549.5 16.0 %copy-start.16 = (s32[128,2]{0,1:T(2,128)S(1)}, s32[128,2]{0,1:T(2,128)}, u32[]{:S(2)}) copy-start(s32[128,2]{0,1:T(2,128)} %param.23) | copy-start | bytes 3076
  549.5 18.0 %copy-start.17 = (s32[6]{0:T(128)S(1)}, s32[6]{0:T(128)}, u32[]{:S(2)}) copy-start(s32[6]{0:T(128)} %param.22) | copy-start | bytes 76
  549.5 18.1 %copy-start.11 = (bf16[8,576]{1,0:T(8,128)(2,1)S(1)}, bf16[8,576]{1,0:T(8,128)(2,1)}, u32[]{:S(2)}) copy-start(bf16[8,576]{1,0:T(8,128)(2,1)} %param.19) | copy-start | bytes 27652
  549.5 18.1 %copy-start.2 = (bf16[8,128,576]{1,2,0:T(8,128)(2,1)S(1)}, bf16[8,128,576]{1,2,0:T(8,128)(2,1)}, u32[]{:S(2)}) copy-start(bf16[8,128,576]{1,2,0:T(8,128)(2,1)} %param.18) | copy-start | bytes 3538948
  549.5 171.5 %all-to-all-start = ((bf16[16,2,256,576]{2,3,1,0:T(8,128)(2,1)}), bf16[16,2,256,576]{2,3,1,0:T(8,128)(2,1)}, u32[]{:S(2)}, u32[]{:S(2)}) async-start(bf16[16,2,256,576]{2,3,1,0:T(8,128)(2,1)} %select_select_fusion), calls=%async_computation | async-start | bytes 18874368 | tf_op jit(solution)/shard_map/all_to_all | solution.py:75
  567.8 2.9 copy-start.18
  722.4 3.7 copy-start.8
  726.1 36.4 %all-to-all-start.4 = ((bf16[16,5,7168]{2,1,0:T(8,128)(2,1)}), bf16[16,5,7168]{2,1,0:T(8,128)(2,1)S(1)}, u32[]{:S(2)}, u32[]{:S(2)}) async-start(bf16[16,5,7168]{2,1,0:T(8,128)(2,1)} %reshape.207), calls=%async_computation.6 | async-start | bytes 3670016 | tf_op jit(solution)/shard_map/all_to_all | solution.py:153
  736.6 1.2 copy-start.10
  736.6 1.4 copy-start.9
  736.7 1.8 copy-start.7
  763.1 4.4 copy-start.1
Sparse Core Ops, SparseCore 0:
  10.7 47.0 all-gather.7
  151.2 91.0 all-gather.9
  244.7 67.1 all-reduce.1
  319.4 74.7 reduce-scatter.2
  437.5 49.2 all-gather.5
  542.0 56.3 reduce-scatter.4
